TPU v7x, 256 devices: a whole 4x4x8 slice. The times are simulated.
256 devices in a mesh: seq: 16 (over x_lo, z), mp: 8 (over y, core), dp: 2 (over x_hi).
Axes of the slice: x: 4 (x_hi: 2, x_lo: 2; x = x_hi * 2 + x_lo), y: 4, z: 8, core: 2. Of those that a mesh axis runs over, the one named last changes fastest.
Arguments:
- residual_in: bfloat16 [12288, 2048], P(('dp', 'seq')), parts along dimension 0, may hold values from -6 to 6
- queries: bfloat16 [12288, 2048], P(('dp', 'seq'), 'mp'), parts along dimension 0, may hold values from -30 to 30
- keys: bfloat16 [12288, 2048], P(('dp', 'seq'), 'mp'), parts along dimension 0, may hold values from -10 to 10
- values: bfloat16 [12288, 2048], P(('dp', 'seq'), 'mp'), parts along dimension 0, may hold values from -6 to 6
- w_out: bfloat16 [2048, 2048], P('mp', 'seq'), may hold values from -0.1875 to 0.1875
- conv_value: bfloat16 [2048, 2048], P('seq', 'mp'), may hold values from -0.125 to 0.125
- conv_gate: bfloat16 [2048, 2048], P('seq', 'mp'), may hold values from -0.125 to 0.125
- depth_kernel: float32 [31, 2048], P(None, 'mp'), may hold values from -2 to 2
- conv_out: bfloat16 [2048, 2048], P('mp', 'seq'), may hold values from -0.25 to 0.25
- ffn_in: bfloat16 [2048, 8192], P('seq', 'mp'), may hold values from -0.125 to 0.125
- ffn_down: bfloat16 [8192, 2048], P('mp', 'seq'), may hold values from -0.1875 to 0.1875
- ffn_mask: int32 [96, 64], P(('dp', 'seq'), 'mp'), parts along dimension 0, may hold values 0 or 1
Outputs:
- block_out: float32 [12288, 2048], P(('dp', 'seq', 'mp')), parts along dimension 0
There are 2 independent parts, one for each index of `dp`. A program takes and returns all parts, laid end to end along the dimension named above; an argument that names none is the same for every part. Nothing has to cross between parts.
All inputs are finite; a program needn't handle non-finite values. No bound on the sum of `ffn_mask` on one device may be relied on, other than what follows from the above.
Results may differ from a plain program's by a relative error of at most 0.017.
Values may be sent and summed in bfloat16 or wider, within the bound.
A program may use at most 128 MiB of HBM per device.

v0:
```python
import math
import jax
import jax.numpy as jnp
from jax import lax
from jax.sharding import PartitionSpec as P

HEAD_DIM = 128
norm_epsilon = 1e-05


def padded_2(value, sides, width):
    for axis, dim in sides:
        count, length = (lax.axis_size(axis), value.shape[dim])
        up = [(i, (i + 1) % count) for i in range(count - 1)]
        down = [(j, i) for i, j in up]
        last = lax.slice_in_dim(value, length - width, length, axis=dim)
        leading = lax.slice_in_dim(value, 0, width, axis=dim)
        before = lax.ppermute(last, axis, up)
        after = lax.ppermute(leading, axis, down)
        value = jnp.concatenate([before, value, after], axis=dim)
    return value


def layer_norm(stream):
    row_mean = jnp.mean(stream, axis=-1, keepdims=True)
    centered = stream - row_mean
    spread = jnp.mean(centered * centered, axis=-1, keepdims=True)
    return centered * lax.rsqrt(spread + norm_epsilon)


def accumulate_rows(left, weight_piece):
    return jnp.dot(left, weight_piece, preferred_element_type=jnp.float32)


def add_branch(stream, branch_part, factor):
    return stream + factor * lax.psum(branch_part.astype(jnp.bfloat16), "mp").astype(jnp.float32)


def on_device(
    residual_in,
    queries,
    keys,
    values,
    w_out,
    conv_value,
    conv_gate,
    depth_kernel,
    conv_out,
    ffn_in,
    ffn_down,
    ffn_mask,
):
    row_count = queries.shape[0]
    local_width = queries.shape[1]
    heads_here = local_width // HEAD_DIM
    score_scale = 1.0 / math.sqrt(HEAD_DIM)
    query_heads = queries.reshape(row_count, heads_here, HEAD_DIM)
    pieces = (
        lax.all_gather(keys, "seq", axis=0, tiled=True),
        lax.all_gather(values, "seq", axis=0, tiled=True),
    )
    running_max = jnp.full((row_count, heads_here), -1e30, jnp.float32)
    key_heads = pieces[0].reshape(pieces[0].shape[0], heads_here, HEAD_DIM)
    value_heads = pieces[1].reshape(pieces[1].shape[0], heads_here, HEAD_DIM)
    scores = (
        jnp.einsum("qhd,khd->qhk", query_heads, key_heads, preferred_element_type=jnp.float32)
        * score_scale
    )
    new_max = jnp.maximum(running_max, jnp.max(scores, axis=-1))
    exp_scores = jnp.exp(scores - new_max[..., None])
    running_sum = jnp.sum(exp_scores, axis=-1)
    weighted = jnp.einsum(
        "qhk,khd->qhd",
        exp_scores.astype(jnp.bfloat16),
        value_heads,
        preferred_element_type=jnp.float32,
    )
    weighted, running_max, running_sum = (weighted, new_max, running_sum)
    heads_out = (
        (weighted / running_sum[..., None]).reshape(row_count, local_width).astype(jnp.bfloat16)
    )
    attn_part = jnp.dot(
        heads_out,
        lax.all_gather(w_out, "seq", axis=1, tiled=True),
        preferred_element_type=jnp.float32,
    )
    share_count = row_count // lax.axis_size("mp")
    stream = residual_in.astype(jnp.float32)
    stream = add_branch(stream, attn_part, 1.0)
    norm_one = layer_norm(stream).astype(jnp.bfloat16)
    conv_width = conv_value.shape[1]
    pieces = (
        lax.all_gather(conv_value, "seq", axis=0, tiled=True),
        lax.all_gather(conv_gate, "seq", axis=0, tiled=True),
    )
    value_half = accumulate_rows(norm_one, pieces[0])
    gate_half = accumulate_rows(norm_one, pieces[1])
    gated_units = (value_half * jax.nn.sigmoid(gate_half)).astype(jnp.bfloat16)
    half_width = depth_kernel.shape[0] // 2
    padded = padded_2(gated_units, (("seq", 0),), half_width)
    depth_out = jnp.zeros((row_count, conv_width), jnp.float32)
    for tap_index in range(depth_kernel.shape[0]):
        depth_out = depth_out + depth_kernel[tap_index] * padded[
            tap_index : tap_index + row_count
        ].astype(jnp.float32)
    activated = jax.nn.silu(depth_out).astype(jnp.bfloat16)
    conv_part = jnp.dot(
        activated,
        lax.all_gather(conv_out, "seq", axis=1, tiled=True),
        preferred_element_type=jnp.float32,
    )
    stream = add_branch(stream, conv_part, 1.0)
    norm_two = layer_norm(stream).astype(jnp.bfloat16)
    pre_hidden = accumulate_rows(norm_two, lax.all_gather(ffn_in, "seq", axis=0, tiled=True))
    tile_count, block_count = ffn_mask.shape
    hidden = (
        jax.nn.silu(pre_hidden).reshape(tile_count, row_count // tile_count, block_count, -1)
        * ffn_mask.astype(jnp.float32)[:, None, :, None]
    )
    hidden = hidden.reshape(row_count, -1).astype(jnp.bfloat16)
    ffn_part = jnp.dot(
        hidden,
        lax.all_gather(ffn_down, "seq", axis=1, tiled=True),
        preferred_element_type=jnp.float32,
    )
    stream = add_branch(stream, ffn_part, 0.5)
    stream = lax.dynamic_slice_in_dim(stream, lax.axis_index("mp") * share_count, share_count, 0)
    return layer_norm(stream)


def solution(mesh):
    in_specs = (
        P(("dp", "seq"), None),
        P(("dp", "seq"), "mp"),
        P(("dp", "seq"), "mp"),
        P(("dp", "seq"), "mp"),
        P("mp", "seq"),
        P("seq", "mp"),
        P("seq", "mp"),
        P(None, "mp"),
        P("mp", "seq"),
        P("seq", "mp"),
        P("mp", "seq"),
        P(("dp", "seq"), "mp"),
    )
    out_specs = P(("dp", "seq", "mp"), None)
    return jax.shard_map(
        on_device, mesh=mesh, in_specs=in_specs, out_specs=out_specs, check_vma=False
    )
```

profile of v0, /device:TPU:2, one launch (start us, length us, event | category | flops | bytes accessed | tf_op | source)
XLA Modules:
  0.0 830.0 jit_solution(12674205064811095764)
XLA Ops:
  9.9 74.6 %all-gather.9.cloned.1.call-done = bf16[6144,256]{0,1:T(8,128)(2,1)} async-done(((bf16[384,256]{0,1:T(8,128)(2,1)}), bf16[6144,256]{0,1:T(8,128)(2,1)}) %all-gather.9.cloned.1.call-update) | async-done | bytes 3145744 | tf_op jit(solution)/shard_map/all_gather | solution.py:59
  84.5 11.3 %bitcast_reduce_fusion = (f32[384,2]{0,1:T(2,128)S(1)}, f32[2,6144,384]{2,1,0:T(8,128)}) fusion(bf16[6144,2,128]{0,2,1:T(8,128)(2,1)} %bitcast.85, bf16[384,256]{1,0:T(8,128)(2,1)S(1)} %copy-done), kind=kOutput, calls=%fused_computation.1 | convolution fusion | flops 1217395968 | bytes 22219776 | tf_op jit(solution)/shard_map/qhd,khd->qhk/dot_general | solution.py:66
  95.8 61.8 %all-gather.11.cloned.1.call-done = bf16[6144,256]{1,0:T(8,128)(2,1)} async-done(((bf16[384,256]{1,0:T(8,128)(2,1)}), bf16[6144,256]{1,0:T(8,128)(2,1)}) %all-gather.11.cloned.1.call-update) | async-done | bytes 3145744 | tf_op jit(solution)/shard_map/all_gather | solution.py:60
  157.6 4.7 copy.19
  162.3 9.4 %fusion.1 = f32[384,2]{0,1:T(2,128)S(1)} fusion(f32[2,6144,384]{2,1,0:T(8,128)} %get-tuple-element.41, f32[384,2]{0,1:T(2,128)S(1)} %broadcast_maximum_fusion), kind=kLoop, calls=%fused_computation.3 | loop fusion | flops 14155008 | bytes 18880512 | tf_op jit(solution)/shard_map/reduce_sum | solution.py:71
  171.7 10.8 %fusion.22 = bf16[384,2,128]{0,2,1:T(8,128)(2,1)S(1)} fusion(bf16[6144,2,128]{0,2,1:T(8,128)(2,1)} %bitcast.84, f32[2,6144,384]{2,1,0:T(8,128)} %get-tuple-element.41, f32[384,2]{0,1:T(2,128)S(1)} %broadcast_maximum_fusion, f32[384,2]{0,1:T(2,128)S(1)} %fusion.1), kind=kOutput, calls=%fused_computation.59 | convolution fusion | flops 1222311936 | bytes 22222848 | tf_op jit(solution)/shard_map/qhk,khd->qhd/dot_general | solution.py:72
  182.6 39.6 %all-gather.13.cloned.1.call-done = bf16[256,2048]{1,0:T(8,128)(2,1)} async-done(((bf16[256,128]{1,0:T(8,128)(2,1)}), bf16[256,2048]{1,0:T(8,128)(2,1)}) %all-gather.13.cloned.1.call-update) | async-done | bytes 1048592 | tf_op jit(solution)/shard_map/all_gather | solution.py:84
  222.2 3.0 convolution_convert_fusion.2
  227.4 67.0 %all-reduce.4.cloned.1.call-done = bf16[384,2048]{1,0:T(8,128)(2,1)} async-done(((bf16[384,2048]{1,0:T(8,128)(2,1)}), bf16[384,2048]{1,0:T(8,128)(2,1)}) %all-reduce.4.cloned.1.call-update) | async-done | bytes 1572880 | tf_op jit(solution)/shard_map/psum | solution.py:36
  294.4 2.0 fusion.7
  298.9 64.7 %all-gather.17.cloned.1.call-done = bf16[2048,256]{1,0:T(8,128)(2,1)} async-done(((bf16[128,256]{1,0:T(8,128)(2,1)}), bf16[2048,256]{1,0:T(8,128)(2,1)}) %all-gather.17.cloned.1.call-update) | async-done | bytes 1048592 | tf_op jit(solution)/shard_map/all_gather | solution.py:94
  363.6 3.0 fusion.14
  366.7 65.0 %all-gather.15.cloned.1.call-done = bf16[2048,256]{1,0:T(8,128)(2,1)} async-done(((bf16[128,256]{1,0:T(8,128)(2,1)}), bf16[2048,256]{1,0:T(8,128)(2,1)}) %all-gather.15.cloned.1.call-update) | async-done | bytes 1048592 | tf_op jit(solution)/shard_map/all_gather | solution.py:93
  431.6 2.4 fusion.18
  434.0 2.5 collective-permute-start
  436.5 5.5 collective-permute-start.1
  442.0 54.1 %all-gather.19.cloned.1.call-done = bf16[256,2048]{1,0:T(8,128)(2,1)} async-done(((bf16[256,128]{1,0:T(8,128)(2,1)}), bf16[256,2048]{1,0:T(8,128)(2,1)}) %all-gather.19.cloned.1.call-update) | async-done | bytes 1048592 | tf_op jit(solution)/shard_map/all_gather | solution.py:109
  496.1 10.9 %convolution_convert_fusion.1 = bf16[384,2048]{1,0:T(8,128)(2,1)} fusion(bf16[256,2048]{1,0:T(8,128)(2,1)} %all-gather.19.cloned.1.call-done, bf16[384,256]{1,0:T(8,128)(2,1)} %copy-done.6, bf16[15,256]{1,0:T(8,128)(2,1)S(1)} %collective-permute-done.1, bf16[15,256]{1,0:T(8,128)(2,1)S(1)} %collective-permute-done, f32[256]{0:T(256)S(1)} %bitcast.117, ...), kind=kOutput, calls=%fused_computation.15 | convolution fusion | flops 421822464 | bytes 2865152 | tf_op jit(solution)/shard_map/dot_general | solution.py:107
  508.4 67.8 %all-reduce.6.cloned.1.call-done = bf16[384,2048]{1,0:T(8,128)(2,1)} async-done(((bf16[384,2048]{1,0:T(8,128)(2,1)}), bf16[384,2048]{1,0:T(8,128)(2,1)}) %all-reduce.6.cloned.1.call-update) | async-done | bytes 1572880 | tf_op jit(solution)/shard_map/psum | solution.py:36
  576.2 2.1 fusion.61
  580.4 72.2 %all-gather.21.cloned.1.call-done = bf16[2048,1024]{1,0:T(8,128)(2,1)} async-done(((bf16[128,1024]{1,0:T(8,128)(2,1)}), bf16[2048,1024]{1,0:T(8,128)(2,1)}) %all-gather.21.cloned.1.call-update) | async-done | bytes 4194320 | tf_op jit(solution)/shard_map/all_gather | solution.py:114
  652.7 87.1 %all-gather.23.cloned.1.call-done = bf16[1024,2048]{1,0:T(8,128)(2,1)} async-done(((bf16[1024,128]{1,0:T(8,128)(2,1)}), bf16[1024,2048]{1,0:T(8,128)(2,1)}) %all-gather.23.cloned.1.call-update) | async-done | bytes 4194320 | tf_op jit(solution)/shard_map/all_gather | solution.py:123
  739.9 9.5 %convolution_convert_fusion = bf16[384,2048]{1,0:T(8,128)(2,1)} fusion(bf16[1024,2048]{1,0:T(8,128)(2,1)} %all-gather.23.cloned.1.call-done, f32[48,8,8,128]{3,2,1,0:T(8,128)S(1)} %bitcast.86, bf16[2048,1024]{1,0:T(8,128)(2,1)} %all-gather.21.cloned.1.call-done, f32[384,2048]{1,0:T(8,128)} %copy-done.3, f32[384]{0:T(512)S(1)} %add_rsqrt_fusion, ...), kind=kOutput, calls=%fused_computation.14 | convolution fusion | flops 3226730496 | bytes 14683136 | tf_op jit(solution)/shard_map/dot_general | solution.py:121
  749.4 69.5 %all-reduce.8.cloned.1.call-done = bf16[384,2048]{1,0:T(8,128)(2,1)} async-done(((bf16[384,2048]{1,0:T(8,128)(2,1)}), bf16[384,2048]{1,0:T(8,128)(2,1)}) %all-reduce.8.cloned.1.call-update) | async-done | bytes 1572880 | tf_op jit(solution)/shard_map/psum | solution.py:36
  (57 shorter events, 16.2 us)
Async XLA Ops:
  6.5 78.0 %copy-start = (bf16[384,256]{1,0:T(8,128)(2,1)S(1)}, bf16[384,256]{1,0:T(8,128)(2,1)}, u32[]{:S(2)}) copy-start(bf16[384,256]{1,0:T(8,128)(2,1)} %param.13) | copy-start | bytes 589828
  6.5 78.0 %all-gather.9.cloned.1.call-start = ((), (), s32[]{:S(2)}) async-start(), calls=%async_computation | async-start | bytes 3342336 | tf_op jit(solution)/shard_map/all_gather | solution.py:59
  8.3 149.3 %all-gather.11.cloned.1.call-start = ((), (), s32[]{:S(2)}) async-start(), calls=%async_computation.1 | async-start | bytes 3342336 | tf_op jit(solution)/shard_map/all_gather | solution.py:60
  9.1 213.1 %all-gather.13.cloned.1.call-start = ((), (), s32[]{:S(2)}) async-start(), calls=%async_computation.2 | async-start | bytes 1114112 | tf_op jit(solution)/shard_map/all_gather | solution.py:84
  9.8 284.6 %all-reduce.4.cloned.1.call-start = ((), (), s32[]{:S(2)}) async-start(), calls=%async_computation.3 | async-start | bytes 3145728 | tf_op jit(solution)/shard_map/psum | solution.py:36
  182.5 44.8 %copy-start.4 = (f32[31,256]{1,0:T(8,128)S(1)}, f32[31,256]{1,0:T(8,128)}, u32[]{:S(2)}) copy-start(f32[31,256]{1,0:T(8,128)} %param.19) | copy-start | bytes 95236
  182.6 111.8 %copy-start.1 = (bf16[384,2048]{1,0:T(8,128)(2,1)S(1)}, bf16[384,2048]{1,0:T(8,128)(2,1)}, u32[]{:S(2)}) copy-start(bf16[384,2048]{1,0:T(8,128)(2,1)} %param.12) | copy-start | bytes 4718596
  225.2 138.4 %all-gather.17.cloned.1.call-start = ((), (), s32[]{:S(2)}) async-start(), calls=%async_computation.5 | async-start | bytes 1114112 | tf_op jit(solution)/shard_map/all_gather | solution.py:94
  225.8 205.8 %all-gather.15.cloned.1.call-start = ((), (), s32[]{:S(2)}) async-start(), calls=%async_computation.4 | async-start | bytes 1114112 | tf_op jit(solution)/shard_map/all_gather | solution.py:93
  226.4 269.7 %all-gather.19.cloned.1.call-start = ((), (), s32[]{:S(2)}) async-start(), calls=%async_computation.6 | async-start | bytes 1114112 | tf_op jit(solution)/shard_map/all_gather | solution.py:109
  227.1 349.0 %all-reduce.6.cloned.1.call-start = ((), (), s32[]{:S(2)}) async-start(), calls=%async_computation.7 | async-start | bytes 3145728 | tf_op jit(solution)/shard_map/psum | solution.py:36
  294.4 2.0 copy-start.2
  434.0 8.0 copy-start.6
  434.0 62.1 %collective-permute-start = (bf16[15,256]{1,0:T(8,128)(2,1)S(1)}, bf16[15,256]{1,0:T(8,128)(2,1)S(1)}, u32[]{:S(2)}, u32[]{:S(2)}) collective-permute-start(bf16[15,256]{1,0:T(8,128)(2,1)S(1)} %get-tuple-element.7), channel_id=1, source_target_pairs={{0,16},{16,32},{32,48},{48,64},{64,80},{80,96},{96,112},{112,128},... | collective-permute-start | bytes 23048 | tf_op jit(solution)/shard_map/ppermute | solution.py:18
  436.5 59.6 %collective-permute-start.1 = (bf16[15,256]{1,0:T(8,128)(2,1)S(1)}, bf16[15,256]{1,0:T(8,128)(2,1)S(1)}, u32[]{:S(2)}, u32[]{:S(2)}) collective-permute-start(bf16[15,256]{1,0:T(8,128)(2,1)S(1)} %get-tuple-element.8), channel_id=1, source_target_pairs={{16,0},{32,16},{48,32},{64,48},{80,64},{96,80},{112,96},{128,112},... | collective-permute-start | bytes 23048 | tf_op jit(solution)/shard_map/ppermute | solution.py:19
  496.1 12.3 %copy-start.5 = (s32[3,8]{1,0:T(4,128)S(1)}, s32[3,8]{1,0:T(4,128)}, u32[]{:S(2)}) copy-start(s32[3,8]{1,0:T(4,128)} %param.23) | copy-start | bytes 292
  507.0 145.7 %all-gather.21.cloned.1.call-start = ((), (), s32[]{:S(2)}) async-start(), calls=%async_computation.8 | async-start | bytes 4456448 | tf_op jit(solution)/shard_map/all_gather | solution.py:114
  507.7 232.0 %all-gather.23.cloned.1.call-start = ((), (), s32[]{:S(2)}) async-start(), calls=%async_computation.9 | async-start | bytes 4456448 | tf_op jit(solution)/shard_map/all_gather | solution.py:123
  508.3 310.6 %all-reduce.8.cloned.1.call-start = ((), (), s32[]{:S(2)}) async-start(), calls=%async_computation.10 | async-start | bytes 3145728 | tf_op jit(solution)/shard_map/psum | solution.py:36
  578.3 1.7 copy-start.3
Sparse Core Ops, SparseCore 0:
  9.1 75.3 all-gather.8
  86.3 71.3 all-gather.10
  159.4 62.7 all-gather.12
  225.3 69.0 all-reduce.3
  296.0 67.5 all-gather.16
  365.3 66.3 all-gather.14
  433.3 62.6 all-gather.18
  507.1 69.0 all-reduce.5
  578.0 74.6 all-gather.20
  654.2 85.4 all-gather.22
  749.5 69.3 all-reduce.7
where the time goes:
time: 830 us
  waiting for transfers between devices  728 us (88%)
  matrix products  50.9 us (6%)
  other arithmetic  21 us (3%)
  between operations  13.4 us (2%)
  starting transfers between devices  8.53 us (1%)
  local copies, waits for them, and re-layouts  8.4 us (1%)
    psum x3, waiting for transfers between devices, add_branch(): lax.psum(branch_part.astype(jnp.bfloat16), 'mp').astype(jnp.float32)  204 us
    all_gather x1, waiting for transfers between devices, on_device(): lax.all_gather(ffn_down, 'seq', axis=1, tiled=True)  87.1 us
    all_gather x1, waiting for transfers between devices, on_device(): lax.all_gather(keys, 'seq', axis=0, tiled=True)  74.6 us
    all_gather x1, waiting for transfers between devices, on_device(): lax.all_gather(ffn_in, 'seq', axis=0, tiled=True)  72.2 us
    all_gather x1, waiting for transfers between devices, on_device(): lax.all_gather(conv_value, 'seq', axis=0, tiled=True)  65 us
    all_gather x1, waiting for transfers between devices, on_device(): lax.all_gather(conv_gate, 'seq', axis=0, tiled=True)  64.7 us
    all_gather x1, waiting for transfers between devices, on_device(): lax.all_gather(values, 'seq', axis=0, tiled=True)  61.8 us
    all_gather x1, waiting for transfers between devices, on_device(): lax.all_gather(conv_out, 'seq', axis=1, tiled=True)  54.1 us
  transfers between devices with their start and end apart: 13, of which 11 were waited for; matrix products, arithmetic and copies ran while one was open for 6% of the time, Pallas kernels for 0%

commit v1 on v0

--- a/solution.py
+++ b/solution.py
@@ -106,7 +106,9 @@
     activated = jax.nn.silu(depth_out).astype(jnp.bfloat16)
     conv_part = jnp.dot(
         activated,
-        lax.all_gather(conv_out, "seq", axis=1, tiled=True),
+        jnp.concatenate(
+            lax.all_to_all(jnp.stack([conv_out] * lax.axis_size("seq")), "seq", 0, 0), axis=1
+        ),
         preferred_element_type=jnp.float32,
     )
     stream = add_branch(stream, conv_part, 1.0)

time: 830 us -> 779 us (0.939)
  waiting for transfers between devices: 728 us -> 671 us
    all_gather x1 -> x0, waiting for transfers between devices: 54.1 us -> none  [on_device(): lax.all_gather(conv_out, 'seq', axis=1, tiled=True)]
where the time goes in v1:
time: 779 us; the launch traced here: 778 us
  waiting for transfers between devices  671 us (86%)
  matrix products  49.8 us (6%)
  other arithmetic  21 us (3%)
  starting transfers between devices  14.9 us (2%)
  between operations  13.7 us (2%)
  local copies, waits for them, and re-layouts  8.09 us (1%)
    psum x3, waiting for transfers between devices, add_branch(): lax.psum(branch_part.astype(jnp.bfloat16), 'mp').astype(jnp.float32)  198 us
    all_gather x1, waiting for transfers between devices, on_device(): lax.all_gather(ffn_down, 'seq', axis=1, tiled=True)  87.2 us
    all_gather x1, waiting for transfers between devices, on_device(): lax.all_gather(keys, 'seq', axis=0, tiled=True)  74.6 us
    all_gather x1, waiting for transfers between devices, on_device(): lax.all_gather(ffn_in, 'seq', axis=0, tiled=True)  72.2 us
    all_gather x1, waiting for transfers between devices, on_device(): lax.all_gather(conv_value, 'seq', axis=0, tiled=True)  65 us
    all_gather x1, waiting for transfers between devices, on_device(): lax.all_gather(conv_gate, 'seq', axis=0, tiled=True)  64.7 us
    all_gather x1, waiting for transfers between devices, on_device(): lax.all_gather(values, 'seq', axis=0, tiled=True)  61.8 us
    all_gather x1, waiting for transfers between devices, on_device(): lax.all_gather(w_out, 'seq', axis=1, tiled=True)  42.1 us
  transfers between devices with their start and end apart: 13, of which 11 were waited for; matrix products, arithmetic and copies ran while one was open for 6% of the time, Pallas kernels for 0%

profile of v1, /device:TPU:2, one launch (start us, length us, event | category | flops | bytes accessed | tf_op | source)
XLA Modules:
  0.0 778.3 jit_solution(5712600199504699896)
XLA Ops:
  9.9 74.6 %all-gather.8.cloned.1.call-done = bf16[6144,256]{0,1:T(8,128)(2,1)} async-done(((bf16[384,256]{0,1:T(8,128)(2,1)}), bf16[6144,256]{0,1:T(8,128)(2,1)}) %all-gather.8.cloned.1.call-update) | async-done | bytes 3145744 | tf_op jit(solution)/shard_map/all_gather | solution.py:59
  84.5 11.3 %bitcast_reduce_fusion = (f32[384,2]{0,1:T(2,128)S(1)}, f32[2,6144,384]{2,1,0:T(8,128)}) fusion(bf16[6144,2,128]{0,2,1:T(8,128)(2,1)} %bitcast.88, bf16[384,256]{1,0:T(8,128)(2,1)S(1)} %copy-done), kind=kOutput, calls=%fused_computation.1 | convolution fusion | flops 1217395968 | bytes 22219776 | tf_op jit(solution)/shard_map/qhd,khd->qhk/dot_general | solution.py:66
  95.8 61.8 %all-gather.10.cloned.1.call-done = bf16[6144,256]{1,0:T(8,128)(2,1)} async-done(((bf16[384,256]{1,0:T(8,128)(2,1)}), bf16[6144,256]{1,0:T(8,128)(2,1)}) %all-gather.10.cloned.1.call-update) | async-done | bytes 3145744 | tf_op jit(solution)/shard_map/all_gather | solution.py:60
  157.6 3.2 copy.19
  160.8 9.4 %fusion.1 = f32[384,2]{0,1:T(2,128)S(1)} fusion(f32[2,6144,384]{2,1,0:T(8,128)} %get-tuple-element.41, f32[384,2]{0,1:T(2,128)S(1)} %broadcast_maximum_fusion), kind=kLoop, calls=%fused_computation.3 | loop fusion | flops 14155008 | bytes 18880512 | tf_op jit(solution)/shard_map/reduce_sum | solution.py:71
  170.3 9.8 %fusion.22 = bf16[384,2,128]{0,2,1:T(8,128)(2,1)S(1)} fusion(bf16[6144,2,128]{0,2,1:T(8,128)(2,1)S(1)} %bitcast.87, f32[2,6144,384]{2,1,0:T(8,128)} %get-tuple-element.41, f32[384,2]{0,1:T(2,128)S(1)} %broadcast_maximum_fusion, f32[384,2]{0,1:T(2,128)S(1)} %fusion.1), kind=kOutput, calls=%fused_computation.59 | convolution fusion | flops 1222311936 | bytes 22222848 | tf_op jit(solution)/shard_map/qhk,khd->qhd/dot_general | solution.py:72
  180.1 42.1 %all-gather.12.cloned.1.call-done = bf16[256,2048]{1,0:T(8,128)(2,1)} async-done(((bf16[256,128]{1,0:T(8,128)(2,1)}), bf16[256,2048]{1,0:T(8,128)(2,1)}) %all-gather.12.cloned.1.call-update) | async-done | bytes 1048592 | tf_op jit(solution)/shard_map/all_gather | solution.py:84
  222.2 3.0 convolution_convert_fusion.2
  227.0 6.4 all-to-all-start
  234.2 60.6 %all-reduce.4.cloned.1.call-done = bf16[384,2048]{1,0:T(8,128)(2,1)} async-done(((bf16[384,2048]{1,0:T(8,128)(2,1)}), bf16[384,2048]{1,0:T(8,128)(2,1)}) %all-reduce.4.cloned.1.call-update) | async-done | bytes 1572880 | tf_op jit(solution)/shard_map/psum | solution.py:36
  294.9 2.0 fusion.7
  299.4 64.7 %all-gather.16.cloned.1.call-done = bf16[2048,256]{1,0:T(8,128)(2,1)} async-done(((bf16[128,256]{1,0:T(8,128)(2,1)}), bf16[2048,256]{1,0:T(8,128)(2,1)}) %all-gather.16.cloned.1.call-update) | async-done | bytes 1048592 | tf_op jit(solution)/shard_map/all_gather | solution.py:94
  364.1 3.0 fusion.14
  367.1 65.0 %all-gather.14.cloned.1.call-done = bf16[2048,256]{1,0:T(8,128)(2,1)} async-done(((bf16[128,256]{1,0:T(8,128)(2,1)}), bf16[2048,256]{1,0:T(8,128)(2,1)}) %all-gather.14.cloned.1.call-update) | async-done | bytes 1048592 | tf_op jit(solution)/shard_map/all_gather | solution.py:93
  432.1 2.4 fusion.18
  434.5 2.5 collective-permute-start
  436.9 5.5 collective-permute-start.1
  443.8 10.8 %convolution_convert_fusion.1 = bf16[384,2048]{1,0:T(8,128)(2,1)} fusion(bf16[256,2048]{0,1:T(8,128)(2,1)} %bitcast.37, bf16[384,256]{1,0:T(8,128)(2,1)} %copy-done.7, bf16[15,256]{1,0:T(8,128)(2,1)S(1)} %collective-permute-done.1, bf16[15,256]{1,0:T(8,128)(2,1)S(1)} %collective-permute-done, f32[256]{0:T(256)S(1)} %bitcast.120, f32[256]{0:T(256)S(1)} %bitcast.121, ...), kind=kOutput, calls=%fused_computation.15 | convolution fusion | flops 421822464 | bytes 2865152 | tf_op jit(solution)/shard_map/dot_general | solution.py:107
  456.2 67.8 %all-reduce.6.cloned.1.call-done = bf16[384,2048]{1,0:T(8,128)(2,1)} async-done(((bf16[384,2048]{1,0:T(8,128)(2,1)}), bf16[384,2048]{1,0:T(8,128)(2,1)}) %all-reduce.6.cloned.1.call-update) | async-done | bytes 1572880 | tf_op jit(solution)/shard_map/psum | solution.py:36
  524.0 2.1 fusion.61
  528.3 72.2 %all-gather.18.cloned.1.call-done = bf16[2048,1024]{1,0:T(8,128)(2,1)} async-done(((bf16[128,1024]{1,0:T(8,128)(2,1)}), bf16[2048,1024]{1,0:T(8,128)(2,1)}) %all-gather.18.cloned.1.call-update) | async-done | bytes 4194320 | tf_op jit(solution)/shard_map/all_gather | solution.py:116
  600.5 87.2 %all-gather.20.cloned.1.call-done = bf16[1024,2048]{1,0:T(8,128)(2,1)} async-done(((bf16[1024,128]{1,0:T(8,128)(2,1)}), bf16[1024,2048]{1,0:T(8,128)(2,1)}) %all-gather.20.cloned.1.call-update) | async-done | bytes 4194320 | tf_op jit(solution)/shard_map/all_gather | solution.py:125
  687.9 9.4 %convolution_convert_fusion = bf16[384,2048]{1,0:T(8,128)(2,1)} fusion(bf16[1024,2048]{1,0:T(8,128)(2,1)} %all-gather.20.cloned.1.call-done, f32[48,8,8,128]{3,2,1,0:T(8,128)S(1)} %bitcast.89, bf16[2048,1024]{1,0:T(8,128)(2,1)} %all-gather.18.cloned.1.call-done, f32[384,2048]{1,0:T(8,128)} %copy-done.3, f32[384]{0:T(512)S(1)} %add_rsqrt_fusion, ...), kind=kOutput, calls=%fused_computation.14 | convolution fusion | flops 3226730496 | bytes 14683136 | tf_op jit(solution)/shard_map/dot_general | solution.py:123
  697.4 69.5 %all-reduce.8.cloned.1.call-done = bf16[384,2048]{1,0:T(8,128)(2,1)} async-done(((bf16[384,2048]{1,0:T(8,128)(2,1)}), bf16[384,2048]{1,0:T(8,128)(2,1)}) %all-reduce.8.cloned.1.call-update) | async-done | bytes 1572880 | tf_op jit(solution)/shard_map/psum | solution.py:36
  (60 shorter events, 18.1 us)
Async XLA Ops:
  6.5 78.0 %copy-start = (bf16[384,256]{1,0:T(8,128)(2,1)S(1)}, bf16[384,256]{1,0:T(8,128)(2,1)}, u32[]{:S(2)}) copy-start(bf16[384,256]{1,0:T(8,128)(2,1)} %param.13) | copy-start | bytes 589828
  6.5 78.0 %all-gather.8.cloned.1.call-start = ((), (), s32[]{:S(2)}) async-start(), calls=%async_computation.1 | async-start | bytes 3342336 | tf_op jit(solution)/shard_map/all_gather | solution.py:59
  8.3 149.3 %all-gather.10.cloned.1.call-start = ((), (), s32[]{:S(2)}) async-start(), calls=%async_computation.2 | async-start | bytes 3342336 | tf_op jit(solution)/shard_map/all_gather | solution.py:60
  9.1 213.1 %all-gather.12.cloned.1.call-start = ((), (), s32[]{:S(2)}) async-start(), calls=%async_computation.3 | async-start | bytes 1114112 | tf_op jit(solution)/shard_map/all_gather | solution.py:84
  9.8 285.0 %all-reduce.4.cloned.1.call-start = ((), (), s32[]{:S(2)}) async-start(), calls=%async_computation.4 | async-start | bytes 3145728 | tf_op jit(solution)/shard_map/psum | solution.py:36
  180.1 45.7 %copy-start.4 = (bf16[256,128]{1,0:T(8,128)(2,1)S(1)}, bf16[256,128]{1,0:T(8,128)(2,1)}, u32[]{:S(2)}) copy-start(bf16[256,128]{1,0:T(8,128)(2,1)} %param.20) | copy-start | bytes 196612
  225.2 9.0 %copy-start.5 = (f32[31,256]{1,0:T(8,128)S(1)}, f32[31,256]{1,0:T(8,128)}, u32[]{:S(2)}) copy-start(f32[31,256]{1,0:T(8,128)} %param.19) | copy-start | bytes 95236
  225.2 69.7 %copy-start.1 = (bf16[384,2048]{1,0:T(8,128)(2,1)S(1)}, bf16[384,2048]{1,0:T(8,128)(2,1)}, u32[]{:S(2)}) copy-start(bf16[384,2048]{1,0:T(8,128)(2,1)} %param.12) | copy-start | bytes 4718596
  225.2 138.9 %all-gather.16.cloned.1.call-start = ((), (), s32[]{:S(2)}) async-start(), calls=%async_computation.6 | async-start | bytes 1114112 | tf_op jit(solution)/shard_map/all_gather | solution.py:94
  227.0 215.5 %all-to-all-start = ((bf16[16,256,128]{1,2,0:T(8,128)(2,1)}), bf16[16,256,128]{1,2,0:T(8,128)(2,1)}, u32[]{:S(2)}, u32[]{:S(2)}) async-start(bf16[16,256,128]{1,2,0:T(8,128)(2,1)} %stack.2), calls=%async_computation | async-start | bytes 2097152 | tf_op jit(solution)/shard_map/all_to_all | solution.py:110
  233.4 198.7 %all-gather.14.cloned.1.call-start = ((), (), s32[]{:S(2)}) async-start(), calls=%async_computation.5 | async-start | bytes 1114112 | tf_op jit(solution)/shard_map/all_gather | solution.py:93
  233.9 290.0 %all-reduce.6.cloned.1.call-start = ((), (), s32[]{:S(2)}) async-start(), calls=%async_computation.7 | async-start | bytes 3145728 | tf_op jit(solution)/shard_map/psum | solution.py:36
  294.9 2.0 copy-start.2
  434.4 8.0 %copy-start.7 = (bf16[384,256]{1,0:T(8,128)(2,1)}, bf16[384,256]{1,0:T(8,128)(2,1)S(1)}, u32[]{:S(2)}) copy-start(bf16[384,256]{1,0:T(8,128)(2,1)S(1)} %fusion.18) | copy-start | bytes 589828
  434.5 8.0 %collective-permute-start = (bf16[15,256]{1,0:T(8,128)(2,1)S(1)}, bf16[15,256]{1,0:T(8,128)(2,1)S(1)}, u32[]{:S(2)}, u32[]{:S(2)}) collective-permute-start(bf16[15,256]{1,0:T(8,128)(2,1)S(1)} %get-tuple-element.7), channel_id=1, source_target_pairs={{0,16},{16,32},{32,48},{48,64},{64,80},{80,96},{96,112},{112,128},... | collective-permute-start | bytes 23048 | tf_op jit(solution)/shard_map/ppermute | solution.py:18
  436.9 6.8 collective-permute-start.1
  443.8 12.4 %copy-start.6 = (s32[3,8]{1,0:T(4,128)S(1)}, s32[3,8]{1,0:T(4,128)}, u32[]{:S(2)}) copy-start(s32[3,8]{1,0:T(4,128)} %param.23) | copy-start | bytes 292
  454.6 145.8 %all-gather.18.cloned.1.call-start = ((), (), s32[]{:S(2)}) async-start(), calls=%async_computation.8 | async-start | bytes 4456448 | tf_op jit(solution)/shard_map/all_gather | solution.py:116
  455.4 232.3 %all-gather.20.cloned.1.call-start = ((), (), s32[]{:S(2)}) async-start(), calls=%async_computation.9 | async-start | bytes 4456448 | tf_op jit(solution)/shard_map/all_gather | solution.py:125
  456.1 310.7 %all-reduce.8.cloned.1.call-start = ((), (), s32[]{:S(2)}) async-start(), calls=%async_computation.10 | async-start | bytes 3145728 | tf_op jit(solution)/shard_map/psum | solution.py:36
  526.1 1.7 copy-start.3
Sparse Core Ops, SparseCore 0:
  9.1 75.3 all-gather.7
  86.3 71.3 all-gather.9
  159.4 62.7 all-gather.11
  225.3 69.4 all-reduce.3
  296.5 67.5 all-gather.15
  365.7 66.3 all-gather.13
  454.8 69.1 all-reduce.5
  525.8 74.6 all-gather.17
  602.2 85.4 all-gather.19
  697.5 69.3 all-reduce.7
